TPU v7x, 128 devices: a whole 4x4x4 slice. The times are simulated.
128 devices in a mesh: sph: 16 (over y_hi, x, core), grp: 8 (over z, y_lo).
Axes of the slice: x: 4, y: 4 (y_hi: 2, y_lo: 2; y = y_hi * 2 + y_lo), z: 4, core: 2. Of those that a mesh axis runs over, the one named last changes fastest.
Arguments:
- pixel_features: bfloat16 [131072, 512], P(('sph', 'grp')), may hold values from -6 to 6
- tier_one_codes: bfloat16 [8192, 512], P(('sph', 'grp')), may hold values from -6 to 6
- tier_two_codes: bfloat16 [512, 512], P(('sph', 'grp')), may hold values from -6 to 6
- tier_three_codes: bfloat16 [32, 512], P('sph'), may hold values from -6 to 6
- tier_one_picks: int32 [8192, 16], P(('sph', 'grp')), may hold values from 0 to 8191, as said below
- tier_two_picks: int32 [8192, 16], P(('sph', 'grp')), may hold values from 0 to 511, as said below
- tier_three_picks: int32 [8192, 16], P(('sph', 'grp')), may hold values from 0 to 31, as said below
- probe_matrix: bfloat16 [3, 512, 512], replicated, may hold values from -0.25 to 0.25
- address_matrix: bfloat16 [3, 512, 512], replicated, may hold values from -0.25 to 0.25
- content_matrix: bfloat16 [3, 512, 512], replicated, may hold values from -0.25 to 0.25
- merge_matrix: bfloat16 [3, 512, 512], replicated, may hold values from -0.25 to 0.25
- expand_matrix: bfloat16 [3, 512, 1024], replicated, may hold values from -0.25 to 0.25
- shrink_matrix: bfloat16 [3, 1024, 512], replicated, may hold values from -0.1875 to 0.1875
- rescale_factors: float32 [3, 3, 512], replicated, may hold values from 0.25 to 1.75
- logit_scaling: float32 [3, 8], replicated, may hold values from 0.5 to 2
Outputs:
- encoded: bfloat16 [131072, 512], P(('sph', 'grp'))
Inputs may be any that keep to these rules, and one draw needn't show every extreme that they name: `tier_one_picks`: entry 0 of block b's list is b, its own level-one parent; every entry lies within 64 of b. `tier_two_picks`: entry 0 of block b's list is b // 16, its level-two parent; every entry lies in the same aligned run of 32 level-two latents as entry 0. `tier_three_picks`: entry 0 of block b's list is b // 256, its level-three parent.
All inputs are finite; a program needn't handle non-finite values.
Results may differ from a plain program's by a relative error of at most 0.01.
Values may be sent and summed in bfloat16 or wider, within the bound.
No kernel may reach another device: no remote copies, remote signals or barrier semaphores. Data moves between devices by JAX's collectives and lax.ppermute only.
A program may use at most 128 MiB of HBM per device.

v0:
```python
import math

import jax
import jax.numpy as jnp
from jax import lax
from jax.sharding import PartitionSpec as P

eps = 1e-06


def with_halo(block, sides, width):
    for axis, dim in sides:
        count = lax.axis_size(axis)
        forward = [(i, i + 1) for i in range(count - 1)]
        backward = [(target, source) for source, target in forward]
        low = lax.ppermute(
            lax.slice_in_dim(block, block.shape[dim] - width, None, axis=dim), axis, forward
        )
        high = lax.ppermute(lax.slice_in_dim(block, 0, width, axis=dim), axis, backward)
        block = jnp.concatenate([low, block, high], axis=dim)
    return block


def normalize(values_in, gain_vec):
    return (
        values_in
        * lax.rsqrt(jnp.mean(values_in * values_in, axis=-1, keepdims=True) + eps)
        * gain_vec
    )


def per_head(values_in, channel_groups):
    dims_shape = values_in.shape
    grouped = values_in.reshape(
        dims_shape[:-1] + (channel_groups, dims_shape[-1] // channel_groups)
    )
    grouped = grouped * lax.rsqrt(jnp.mean(grouped * grouped, axis=-1, keepdims=True) + eps)
    return grouped.reshape(dims_shape)


def refresh(latent, tier_ordinal, expand_matrix, shrink_matrix, rescale_factors):
    running_features = latent.astype(jnp.float32)
    mlp_in = normalize(running_features, rescale_factors[tier_ordinal, 1]).astype(jnp.bfloat16)
    hidden = jax.nn.silu(
        jnp.dot(mlp_in, expand_matrix[tier_ordinal], preferred_element_type=jnp.float32)
    ).astype(jnp.bfloat16)
    renewed = (
        running_features
        + jnp.dot(hidden, shrink_matrix[tier_ordinal], preferred_element_type=jnp.float32)
    ).astype(jnp.bfloat16)
    return lax.optimization_barrier(renewed)


def project(renewed, tier_ordinal, address_matrix, content_matrix, rescale_factors, channel_groups):
    kv_in = normalize(renewed.astype(jnp.float32), rescale_factors[tier_ordinal, 2]).astype(
        jnp.bfloat16
    )
    key_part = per_head(
        jnp.dot(kv_in, address_matrix[tier_ordinal], preferred_element_type=jnp.float32),
        channel_groups,
    ).astype(jnp.bfloat16)
    value_part = jnp.dot(
        kv_in, content_matrix[tier_ordinal], preferred_element_type=jnp.float32
    ).astype(jnp.bfloat16)
    return jnp.concatenate([key_part, value_part], axis=1)


def mix_across_tiers(
    running_features,
    gather_entries,
    tier_positions,
    tier_ordinal,
    probe_matrix,
    merge_matrix,
    rescale_factors,
    logit_scaling,
):
    row_count, feature = running_features.shape
    blocks = tier_positions.shape[0]
    channel_groups = logit_scaling.shape[1]
    group_dimension = feature // channel_groups
    table_rows = gather_entries.shape[0]
    normed = normalize(running_features, rescale_factors[tier_ordinal, 0]).astype(jnp.bfloat16)
    probe_heads = probe_matrix[tier_ordinal].reshape(feature, channel_groups, group_dimension)
    queries = jnp.einsum("rc,chd->hrd", normed, probe_heads, preferred_element_type=jnp.float32)
    queries = queries * lax.rsqrt(jnp.mean(queries * queries, axis=-1, keepdims=True) + eps)
    queries = queries.astype(jnp.bfloat16).reshape(
        channel_groups, blocks, row_count // blocks, group_dimension
    )
    key_heads = jnp.transpose(
        gather_entries[:, :feature].reshape(table_rows, channel_groups, group_dimension), (1, 0, 2)
    )
    value_heads = jnp.transpose(
        gather_entries[:, feature:].reshape(table_rows, channel_groups, group_dimension), (1, 0, 2)
    )
    key_picked = jnp.take(key_heads, tier_positions, axis=1)
    value_picked = jnp.take(value_heads, tier_positions, axis=1)
    affinity_logits = jnp.einsum(
        "hbid,hbjd->hbij", queries, key_picked, preferred_element_type=jnp.float32
    )
    affinity_logits = (
        affinity_logits
        * (logit_scaling[tier_ordinal] / math.sqrt(group_dimension))[:, None, None, None]
    )
    weights = jnp.exp(affinity_logits)
    weights = (weights / jnp.sum(weights, axis=-1, keepdims=True)).astype(jnp.bfloat16)
    mixture = jnp.einsum(
        "hbij,hbjd->hbid", weights, value_picked, preferred_element_type=jnp.float32
    )
    mixture = mixture.astype(jnp.bfloat16).reshape(channel_groups, row_count, group_dimension)
    merge_heads = merge_matrix[tier_ordinal].reshape(channel_groups, group_dimension, feature)
    return running_features + jnp.einsum(
        "hrd,hde->re", mixture, merge_heads, preferred_element_type=jnp.float32
    )


def per_device(
    pixel_features,
    tier_one_codes,
    tier_two_codes,
    tier_three_codes,
    tier_one_picks,
    tier_two_picks,
    tier_three_picks,
    probe_matrix,
    address_matrix,
    content_matrix,
    merge_matrix,
    expand_matrix,
    shrink_matrix,
    rescale_factors,
    logit_scaling,
):
    channel_groups = logit_scaling.shape[1]
    block_count = tier_one_codes.shape[0]
    device_index = lax.axis_index(("sph", "grp"))
    sphere_index = lax.axis_index("sph")
    renewed_one = refresh(tier_one_codes, 0, expand_matrix, shrink_matrix, rescale_factors)
    renewed_two = refresh(tier_two_codes, 1, expand_matrix, shrink_matrix, rescale_factors)
    renewed_three = refresh(tier_three_codes, 2, expand_matrix, shrink_matrix, rescale_factors)
    first_table = with_halo(
        project(renewed_one, 0, address_matrix, content_matrix, rescale_factors, channel_groups),
        ((("sph", "grp"), 0),),
        block_count,
    )
    second_table = lax.all_gather(
        project(renewed_two, 1, address_matrix, content_matrix, rescale_factors, channel_groups),
        "grp",
        axis=0,
        tiled=True,
    )
    third_table = lax.all_gather(
        project(renewed_three, 2, address_matrix, content_matrix, rescale_factors, channel_groups),
        "sph",
        axis=0,
        tiled=True,
    )
    local_first = tier_one_picks - (device_index * block_count - block_count)
    local_second = tier_two_picks - sphere_index * second_table.shape[0]
    running_features = pixel_features.astype(jnp.float32)
    running_features = mix_across_tiers(
        running_features,
        first_table,
        local_first,
        0,
        probe_matrix,
        merge_matrix,
        rescale_factors,
        logit_scaling,
    )
    running_features = mix_across_tiers(
        running_features,
        second_table,
        local_second,
        1,
        probe_matrix,
        merge_matrix,
        rescale_factors,
        logit_scaling,
    )
    running_features = mix_across_tiers(
        running_features,
        third_table,
        tier_three_picks,
        2,
        probe_matrix,
        merge_matrix,
        rescale_factors,
        logit_scaling,
    )
    return running_features.astype(jnp.bfloat16)


def solution(mesh):
    placed = (
        P(("sph", "grp"), None),
        P(("sph", "grp"), None),
        P(("sph", "grp"), None),
        P("sph", None),
        P(("sph", "grp"), None),
        P(("sph", "grp"), None),
        P(("sph", "grp"), None),
        P(),
        P(),
        P(),
        P(),
        P(),
        P(),
        P(),
        P(),
    )
    return jax.shard_map(
        per_device, mesh=mesh, in_specs=placed, out_specs=P(("sph", "grp"), None), check_vma=False
    )
```

profile of v0, /device:TPU:0, one launch (start us, length us, event | category | flops | bytes accessed | tf_op | source)
XLA Modules:
  0.0 173.5 jit_solution(10570810775063675648)
XLA Ops:
  0.0 1.5 fusion.159
  1.6 1.0 fusion.86
  2.5 2.1 %fusion.35 = bf16[64,512]{1,0:T(8,128)(2,1)S(1)} fusion(bf16[3,1024,512]{2,1,0:T(8,128)(2,1)} %param.31, bf16[3,512,1024]{2,1,0:T(8,128)(2,1)} %param.30, bf16[64,512]{1,0:T(8,128)(2,1)} %param.20, f32[512]{0:T(512)S(1)} %bitcast.234, f32[64]{0:T(128)S(1)} %add_rsqrt_fusion.14), kind=kOutput, calls=%fused_computation.63 | convolution fusion | flops 134774784 | bytes 2296064 | tf_op jit(solution)/shard_map/dot_general | solution.py:49
  4.8 1.1 slice_bitcast_fusion
  5.9 0.2 copy.141
  6.1 0.4 multiply_reduce_fusion.5
  6.6 1.3 convolution_convert_fusion
  7.9 3.6 %collective-permute-start = (bf16[64,1024]{1,0:T(8,128)(2,1)S(1)}, bf16[64,1024]{1,0:T(8,128)(2,1)S(1)}, u32[]{:S(2)}, u32[]{:S(2)}) collective-permute-start(bf16[64,1024]{1,0:T(8,128)(2,1)S(1)} %pad_maximum_fusion.1), channel_id=1, source_target_pairs={{0,1},{1,2},{2,3},{3,4},{4,5},{5,6},{6,7},{7,8},{8,9},{9,10},{10,1... | collective-permute-start | bytes 393224 | tf_op jit(solution)/shard_map/ppermute | solution.py:16
  11.5 1.3 collective-permute-start.1
  12.8 0.6 compare_select_fusion
  13.4 0.6 compare_and_fusion
  14.3 0.5 copy.136
  14.8 0.2 fusion.3
  15.1 1.9 %multiply_reduce_fusion.4 = (f32[8,1024]{1,0:T(8,128)S(1)}, f32[1024,512]{0,1:S(1)}) fusion(bf16[1024,512]{0,1:T(8,128)(2,1)S(1)} %copy.136, f32[512]{0:T(512)S(1)} %bitcast.233, f32[1024]{0:T(1024)S(1)} %add_rsqrt_fusion.8, bf16[3,512,512]{2,1,0:T(8,128)(2,1)} %param.26), kind=kOutput, calls=%fused_computation.54 | convolution fusion | flops 540008448 | bytes 3708928
  17.1 0.3 multiply_convert_fusion.4
  17.4 1.1 copy.139
  18.5 2.7 %fusion.155 = (bf16[1,512,512]{2,1,0:T(8,128)(2,1)}, bf16[1,512,512]{2,1,0:T(8,128)(2,1)}, bf16[1,512,512]{2,1,0:T(8,128)(2,1)}) fusion(bf16[3,512,512]{2,1,0:T(8,128)(2,1)} %param.29), kind=kLoop, calls=%fused_computation.208 | loop fusion | bytes 3145728 | tf_op jit(solution)/shard_map/slice | solution.py:111
  21.3 2.0 %fusion.36 = bf16[4,512]{1,0:T(4,128)(2,1)S(1)} fusion(bf16[3,1024,512]{2,1,0:T(8,128)(2,1)} %param.31, bf16[3,512,1024]{2,1,0:T(8,128)(2,1)} %param.30, bf16[4,512]{1,0:T(4,128)(2,1)S(1)} %copy-done.21, f32[512]{0:T(512)S(1)} %bitcast.232, f32[4]{0:T(128)S(1)} %add_rsqrt_fusion.12), kind=kOutput, calls=%fused_computation.66 | convolution fusion | flops 8423424 | bytes 2112000 | tf_op jit(solution)/shard_map/dot_general | solution.py:49
  23.3 0.1 fusion.107
  23.4 0.5 add_rsqrt_fusion.11
  23.9 0.2 copy.158
  24.1 1.3 convolution_convert_fusion.1
  25.4 1.1 multiply_reduce_fusion.6
  26.7 31.6 %all-gather = bf16[8,4,1024]{2,1,0:T(4,128)(2,1)S(1)} all-gather(bf16[1,4,1024]{2,1,0:T(4,128)(2,1)S(1)} %maximum_bitcast_fusion), channel_id=1, replica_groups=mesh['sph'=16,'grp'=8] {'grp'}, dimensions={0}, use_global_device_ids=true | all-gather | bytes 73728 | tf_op jit(solution)/shard_map/all_gather | solution.py:146
  58.4 0.7 compare_and_fusion.1
  59.3 0.7 copy.157
  60.1 7.6 %gather_fusion.2 = bf16[1024,8,64]{2,1,0:T(8,128)(2,1)} fusion(bf16[8,32,64]{2,0,1:T(8,128)(2,1)S(1)} %bitcast.199, s32[1024]{0:T(1024)S(1)} %broadcast_clamp_fusion.1), kind=kCustom, calls=%fused_computation.1.clone | custom fusion | bytes 2101248 | tf_op jit(solution)/shard_map/jit(_take)/gather | solution.py:96
  67.7 7.6 %gather_fusion.3 = bf16[1024,8,64]{2,1,0:T(8,128)(2,1)} fusion(bf16[8,32,64]{2,0,1:T(8,128)(2,1)S(1)} %bitcast.201, s32[1024]{0:T(1024)S(1)} %broadcast_clamp_fusion.1), kind=kCustom, calls=%fused_computation.3.clone | custom fusion | bytes 2101248 | tf_op jit(solution)/shard_map/jit(_take)/gather | solution.py:97
  75.5 2.0 %fusion.37 = bf16[2,512]{1,0:T(2,128)(2,1)S(1)} fusion(bf16[3,1024,512]{2,1,0:T(8,128)(2,1)} %param.31, bf16[3,512,1024]{2,1,0:T(8,128)(2,1)} %param.30, bf16[2,512]{1,0:T(2,128)(2,1)S(1)} %copy-done.24, f32[2]{0:T(128)S(1)} %add_rsqrt_fusion.10, f32[512]{0:T(512)S(1)} %bitcast.231), kind=kOutput, calls=%fused_computation.69 | convolution fusion | flops 4211712 | bytes 2105856 | tf_op jit(solution)/shard_map/dot_general | solution.py:49
  77.5 0.1 fusion.123
  77.6 0.5 add_rsqrt_fusion.9
  78.1 0.2 copy.171
  78.4 1.3 convolution_convert_fusion.2
  79.6 1.1 multiply_reduce_fusion.7
  80.9 25.1 %all-gather.1 = bf16[16,2,1024]{2,1,0:T(2,128)(2,1)S(1)} all-gather(bf16[1,2,1024]{2,1,0:T(2,128)(2,1)S(1)} %maximum_bitcast_fusion.1), channel_id=1, replica_groups=mesh['sph'=16,'grp'=8] {'sph'}, dimensions={0}, use_global_device_ids=true | all-gather | bytes 69632 | tf_op jit(solution)/shard_map/all_gather | solution.py:152
  106.2 0.8 copy.173
  107.1 1.4 copy.170
  108.5 7.6 %gather_fusion.4 = bf16[1024,8,64]{2,1,0:T(8,128)(2,1)} fusion(bf16[8,32,64]{2,0,1:T(8,128)(2,1)S(1)} %bitcast.200, s32[1024]{0:T(1024)S(1)} %broadcast_clamp_fusion), kind=kCustom, calls=%fused_computation.4.clone | custom fusion | bytes 2101248 | tf_op jit(solution)/shard_map/jit(_take)/gather | solution.py:96
  116.1 7.6 %gather_fusion.5 = bf16[1024,8,64]{2,1,0:T(8,128)(2,1)} fusion(bf16[8,32,64]{2,0,1:T(8,128)(2,1)S(1)} %bitcast.202, s32[1024]{0:T(1024)S(1)} %broadcast_clamp_fusion), kind=kCustom, calls=%fused_computation.5.clone | custom fusion | bytes 2101248 | tf_op jit(solution)/shard_map/jit(_take)/gather | solution.py:97
  123.7 0.5 multiply_bitcast_fusion
  124.2 0.9 pad_maximum_fusion
  125.2 0.1 copy.148
  125.4 0.2 copy.149
  125.6 0.1 copy.143
  125.7 0.2 copy.144
  126.0 7.6 %gather_fusion.1 = bf16[1024,8,64]{2,1,0:T(8,128)(2,1)} fusion(bf16[8,192,64]{2,0,1:T(8,128)(2,1)S(1)} %bitcast.203, s32[1024]{0:T(1024)S(1)} %broadcast_clamp_fusion.2), kind=kCustom, calls=%fused_computation.2.clone | custom fusion | bytes 2101248 | tf_op jit(solution)/shard_map/jit(_take)/gather | solution.py:97
  133.6 7.6 %gather_fusion = bf16[1024,8,64]{2,1,0:T(8,128)(2,1)} fusion(bf16[8,192,64]{2,0,1:T(8,128)(2,1)S(1)} %bitcast.204, s32[1024]{0:T(1024)S(1)} %broadcast_clamp_fusion.2), kind=kCustom, calls=%fused_computation.clone | custom fusion | bytes 2101248 | tf_op jit(solution)/shard_map/jit(_take)/gather | solution.py:96
  141.2 3.5 %select_bitcast_fusion.1 = (bf16[8,64,16,64]{3,0,2,1:T(8,128)(2,1)S(1)}, bf16[8,64,16,64]{3,0,2,1:T(8,128)(2,1)S(1)}) fusion(bf16[64,16,8,64]{3,2,1,0:T(8,128)(2,1)} %bitcast.207, pred[64,16]{1,0:T(8,128)(4,1)S(1)} %copy.140, bf16[64,16,8,64]{3,2,1,0:T(8,128)(2,1)} %bitcast.206), kind=kLoop, calls=%fused_computation.41 | loop fusion | flops 1048576 | bytes 4195328 | tf_op jit(solution)/shard_map/jit(_take)/select_n | solution.py:96
  144.8 1.4 fusion
  146.2 1.6 fusion.26
  147.9 1.3 multiply_reduce_fusion.3
  149.3 2.3 %multiply_reduce_fusion.2 = (f32[8,1024]{1,0:T(8,128)S(1)}, f32[1024,512]{0,1:S(1)}) fusion(f32[1024,512]{0,1:T(8,128)S(1)} %get-tuple-element.46, f32[512]{0:T(512)S(1)} %bitcast.224, f32[1024]{0:T(1024)S(1)} %add_rsqrt_fusion.6, bf16[3,512,512]{2,1,0:T(8,128)(2,1)} %param.26), kind=kOutput, calls=%fused_computation.49 | convolution fusion | flops 539484160 | bytes 4757504
  151.6 0.3 multiply_convert_fusion.2
  151.9 1.1 copy.156
  153.0 4.3 %fusion.1 = (f32[8,64,16]{2,1,0:T(8,128)S(1)}, f32[8,64,16,16]{2,3,1,0:T(8,128)S(1)}) fusion(f32[8]{0:T(128)S(1)} %copy-done.27, bf16[8,64,16,64]{3,2,1,0:T(8,128)(2,1)S(1)} %bitcast.209, bf16[64,16,8,64]{3,2,1,0:T(8,128)(2,1)} %bitcast.212, pred[64,16]{1,0:T(8,128)(4,1)S(1)} %copy-done.19), kind=kOutput, calls=%fused_computation.13 | convolution fusion | flops 17555456 | bytes 2655264 | tf_op jit(solution)/shard_map/hbid,hbjd->hbij/dot_general | solution.py:98
  157.4 2.1 %fusion.29 = bf16[8,64,16,64]{3,2,1,0:T(8,128)(2,1)S(1)} fusion(bf16[64,16,8,64]{3,2,1,0:T(8,128)(2,1)S(1)} %bitcast.211, pred[64,16]{1,0:T(8,128)(4,1)S(1)} %copy-done.19, f32[8,64,16,16]{2,3,1,0:T(8,128)S(1)} %get-tuple-element.50, f32[8,64,16]{2,1,0:T(8,128)S(1)} %get-tuple-element.49, f32[8]{0:T(128)S(1)} %copy-done.27), kind=kOutput, calls=%fused_computation.60 | convolution fusion | flops 18219008 | bytes 2655264 | tf_op jit(solution)/shard_map/hbij,hbjd->hbid/dot_general | solution.py:107
  159.5 1.3 multiply_reduce_fusion.1
  160.8 1.9 %multiply_reduce_fusion = (f32[8,1024]{1,0:T(8,128)S(1)}, f32[1024,512]{0,1:S(1)}) fusion(f32[1024,512]{0,1:T(8,128)S(1)} %get-tuple-element.54, f32[512]{0:T(512)S(1)} %bitcast.223, f32[1024]{0:T(1024)S(1)} %add_rsqrt_fusion.4, bf16[3,512,512]{2,1,0:T(8,128)(2,1)} %param.26), kind=kOutput, calls=%fused_computation.44 | convolution fusion | flops 539484160 | bytes 4757504
  162.7 0.3 multiply_convert_fusion
  163.0 1.8 %copy.169 = bf16[8,1024,64]{2,1,0:T(8,128)(2,1)} copy(bf16[8,1024,64]{1,2,0:T(8,128)(2,1)S(1)} %multiply_convert_fusion) | data formatting | bytes 2097152 | tf_op jit(solution)/shard_map/convert_element_type | solution.py:87
  164.8 3.9 %fusion.2 = (f32[8,64,16]{2,1,0:T(8,128)S(1)}, f32[8,64,16,16]{2,3,1,0:T(8,128)S(1)}) fusion(f32[8]{0:T(128)S(1)} %copy-done.26, bf16[8,64,16,64]{3,2,1,0:T(8,128)(2,1)} %bitcast.208, bf16[64,16,8,64]{3,2,1,0:T(8,128)(2,1)} %bitcast.214, pred[64,16]{1,0:T(8,128)(4,1)S(1)} %copy-done.20), kind=kOutput, calls=%fused_computation.14 | convolution fusion | flops 17555456 | bytes 2655264 | tf_op jit(solution)/shard_map/hbid,hbjd->hbij/dot_general | solution.py:98
  168.8 2.1 %fusion.32 = bf16[8,64,16,64]{3,2,1,0:T(8,128)(2,1)S(1)} fusion(bf16[64,16,8,64]{3,2,1,0:T(8,128)(2,1)S(1)} %bitcast.213, pred[64,16]{1,0:T(8,128)(4,1)S(1)} %copy-done.20, f32[8,64,16,16]{2,3,1,0:T(8,128)S(1)} %get-tuple-element.58, f32[8,64,16]{2,1,0:T(8,128)S(1)} %get-tuple-element.57, f32[8]{0:T(128)S(1)} %copy-done.26), kind=kOutput, calls=%fused_computation.61 | convolution fusion | flops 18219008 | bytes 2655264 | tf_op jit(solution)/shard_map/hbij,hbjd->hbid/dot_general | solution.py:107
  170.9 1.3 fusion.6
  172.2 1.3 copy.181
  (104 shorter events, 2.1 us)
Async XLA Ops:
  0.0 4.8 %copy-start.8 = (bf16[3,512,512]{2,1,0:T(8,128)(2,1)S(1)}, bf16[3,512,512]{2,1,0:T(8,128)(2,1)}, u32[]{:S(2)}) copy-start(bf16[3,512,512]{2,1,0:T(8,128)(2,1)} %param.27) | copy-start | bytes 4718596
  5.8 7.0 %copy-start.13 = (s32[64,16]{0,1:T(8,128)S(1)}, s32[64,16]{0,1:T(8,128)}, u32[]{:S(2)}) copy-start(s32[64,16]{0,1:T(8,128)} %param.25) | copy-start | bytes 12292
  5.9 8.2 %copy-start.18 = (s32[64,16]{0,1:T(8,128)S(1)}, s32[64,16]{0,1:T(8,128)}, u32[]{:S(2)}) copy-start(s32[64,16]{0,1:T(8,128)} %param.23) | copy-start | bytes 12292
  5.9 8.4 %copy-start.9 = (bf16[1024,512]{1,0:T(8,128)(2,1)S(1)}, bf16[1024,512]{1,0:T(8,128)(2,1)}, u32[]{:S(2)}) copy-start(bf16[1024,512]{1,0:T(8,128)(2,1)} %param.19) | copy-start | bytes 3145732
  7.9 116.3 %collective-permute-start = (bf16[64,1024]{1,0:T(8,128)(2,1)S(1)}, bf16[64,1024]{1,0:T(8,128)(2,1)S(1)}, u32[]{:S(2)}, u32[]{:S(2)}) collective-permute-start(bf16[64,1024]{1,0:T(8,128)(2,1)S(1)} %pad_maximum_fusion.1), channel_id=1, source_target_pairs={{0,1},{1,2},{2,3},{3,4},{4,5},{5,6},{6,7},{7,8},{8,9},{9,10},{10,1... | collective-permute-start | bytes 393224 | tf_op jit(solution)/shard_map/ppermute | solution.py:16
  11.5 112.7 %collective-permute-start.1 = (bf16[64,1024]{1,0:T(8,128)(2,1)S(1)}, bf16[64,1024]{1,0:T(8,128)(2,1)}, u32[]{:S(2)}, u32[]{:S(2)}) collective-permute-start(bf16[64,1024]{1,0:T(8,128)(2,1)S(1)} %pad_maximum_fusion.1), channel_id=1, source_target_pairs={{1,0},{2,1},{3,2},{4,3},{5,4},{6,5},{7,6},{8,7},{9,8},{10,9},{11,1... | collective-permute-start | bytes 393224 | tf_op jit(solution)/shard_map/ppermute | solution.py:19
  14.8 2.2 %copy-start = (bf16[1024,512]{0,1:T(8,128)(2,1)}, bf16[1024,512]{0,1:T(8,128)(2,1)S(1)}, u32[]{:S(2)}) copy-start(bf16[1024,512]{0,1:T(8,128)(2,1)S(1)} %copy.136) | copy-start | bytes 3145732
  18.5 2.7 %copy-start.21 = (bf16[4,512]{1,0:T(4,128)(2,1)S(1)}, bf16[4,512]{1,0:T(4,128)(2,1)}, u32[]{:S(2)}) copy-start(bf16[4,512]{1,0:T(4,128)(2,1)} %param.21) | copy-start | bytes 12292
  18.5 2.8 %copy-start.23 = (f32[1,1,512]{2,1,0:T(1,128)S(1)}, f32[1,1,512]{2,1,0:T(1,128)}, u32[]{:S(2)}) copy-start(f32[1,1,512]{2,1,0:T(1,128)} %get-tuple-element.25) | copy-start | bytes 6148
  18.5 5.4 %copy-start.7 = (bf16[512,512]{0,1:T(8,128)(2,1)S(1)}, bf16[512,512]{0,1:T(8,128)(2,1)}, u32[]{:S(2)}) copy-start(bf16[512,512]{0,1:T(8,128)(2,1)} %get-tuple-element.16) | copy-start | bytes 1572868
  67.7 7.6 %copy-start.24 = (bf16[2,512]{1,0:T(2,128)(2,1)S(1)}, bf16[2,512]{1,0:T(2,128)(2,1)}, u32[]{:S(2)}) copy-start(bf16[2,512]{1,0:T(2,128)(2,1)} %param.22) | copy-start | bytes 6148
  67.7 7.7 %copy-start.22 = (f32[1,1,512]{2,1,0:T(1,128)S(1)}, f32[1,1,512]{2,1,0:T(1,128)}, u32[]{:S(2)}) copy-start(f32[1,1,512]{2,1,0:T(1,128)} %get-tuple-element.31) | copy-start | bytes 6148
  75.3 2.8 %copy-start.6 = (bf16[512,512]{0,1:T(8,128)(2,1)S(1)}, bf16[512,512]{0,1:T(8,128)(2,1)}, u32[]{:S(2)}) copy-start(bf16[512,512]{0,1:T(8,128)(2,1)} %get-tuple-element.14) | copy-start | bytes 1572868
  75.3 3.0 %copy-start.16 = (f32[1,1,512]{2,1,0:T(1,128)S(1)}, f32[1,1,512]{2,1,0:T(1,128)}, u32[]{:S(2)}) copy-start(f32[1,1,512]{2,1,0:T(1,128)} %get-tuple-element.30) | copy-start | bytes 6148
  77.5 0.7 copy-start.17
  116.1 7.6 %copy-start.25 = (f32[3,8]{1,0:T(4,128)S(1)}, f32[3,8]{1,0:T(4,128)}, u32[]{:S(2)}) copy-start(f32[3,8]{1,0:T(4,128)} %param.33) | copy-start | bytes 292
  146.2 1.7 copy-start.1
  146.2 1.7 copy-start.12
  147.9 1.4 copy-start.15
  149.3 2.3 %copy-start.2 = (f32[1024,512]{0,1:T(8,128)}, f32[1024,512]{0,1:T(8,128)S(1)}, u32[]{:S(2)}) copy-start(f32[1024,512]{0,1:T(8,128)S(1)} %get-tuple-element.46) | copy-start | bytes 6291460
  151.9 1.1 copy-start.19
  151.9 1.1 copy-start.27
  153.0 4.3 %copy-start.4 = (bf16[1024,8,64]{2,1,0:T(8,128)(2,1)S(1)}, bf16[1024,8,64]{2,1,0:T(8,128)(2,1)}, u32[]{:S(2)}) copy-start(bf16[1024,8,64]{2,1,0:T(8,128)(2,1)} %gather_fusion.3) | copy-start | bytes 3145732
  157.3 2.1 %copy-start.3 = (f32[1024,512]{0,1:T(8,128)S(1)}, f32[1024,512]{0,1:T(8,128)}, u32[]{:S(2)}) copy-start(f32[1024,512]{0,1:T(8,128)} %copy-done.2) | copy-start | bytes 6291460
  157.3 2.1 %copy-start.11 = (bf16[1,512,512]{2,1,0:T(8,128)(2,1)S(1)}, bf16[1,512,512]{2,1,0:T(8,128)(2,1)}, u32[]{:S(2)}) copy-start(bf16[1,512,512]{2,1,0:T(8,128)(2,1)} %get-tuple-element.13) | copy-start | bytes 1572868
  159.5 1.4 copy-start.14
  163.0 1.9 %copy-start.20 = (pred[64,16]{1,0:T(8,128)(4,1)S(1)}, pred[64,16]{1,0:T(8,128)(4,1)}, u32[]{:S(2)}) copy-start(pred[64,16]{1,0:T(8,128)(4,1)} %copy.170) | copy-start | bytes 3076
  163.0 1.8 %copy-start.26 = (f32[8]{0:T(128)S(1)}, f32[8]{0:T(128)}, u32[]{:S(2)}) copy-start(f32[8]{0:T(128)} %get-tuple-element.34) | copy-start | bytes 100
  164.8 3.9 %copy-start.5 = (bf16[1024,8,64]{2,1,0:T(8,128)(2,1)S(1)}, bf16[1024,8,64]{2,1,0:T(8,128)(2,1)}, u32[]{:S(2)}) copy-start(bf16[1024,8,64]{2,1,0:T(8,128)(2,1)} %gather_fusion.5) | copy-start | bytes 3145732
  168.8 2.1 %copy-start.10 = (bf16[1,512,512]{2,1,0:T(8,128)(2,1)S(1)}, bf16[1,512,512]{2,1,0:T(8,128)(2,1)}, u32[]{:S(2)}) copy-start(bf16[1,512,512]{2,1,0:T(8,128)(2,1)} %get-tuple-element.11) | copy-start | bytes 1572868
where the time goes:
time: 175 us; the launch traced here: 174 us
  local copies, waits for them, and re-layouts  62.3 us (36%)
  blocking collectives  56.7 us (32%)
  matrix products  37.9 us (22%)
  other arithmetic  11 us (6%)
  starting transfers between devices  4.89 us (3%)
    all_gather x1, blocking collectives, per_device(): lax.all_gather(project(renewed_two, 1, address_matrix, content_matrix, re...  31.6 us
    all_gather x1, blocking collectives, per_device(): lax.all_gather(project(renewed_three, 2, address_matrix, content_matrix,...  25.1 us
    gather x3, local copies, waits for them, and re-layouts, mix_across_tiers(): key_picked = jnp.take(key_heads, tier_positions, axis=1)  22.8 us
    gather x3, local copies, waits for them, and re-layouts, mix_across_tiers(): value_picked = jnp.take(value_heads, tier_positions, axis=1)  22.8 us
    dot_general x3, matrix products, mix_across_tiers(): jnp.einsum('hbid,hbjd->hbij', queries, key_picked, preferred_element_type...  9.67 us
    dot_general x3, matrix products, refresh(): jnp.dot(hidden, shrink_matrix[tier_ordinal], preferred_element_type=jnp.f...  6.09 us
    unnamed x3, matrix products  6.07 us
    dot_general x3, matrix products, mix_across_tiers(): jnp.einsum('hbij,hbjd->hbid', weights, value_picked, preferred_element_ty...  5.8 us
  transfers between devices with their start and end apart: 2, of which 0 were waited for; matrix products, arithmetic and copies ran while one was open for 31% of the time, Pallas kernels for 0%

commit v1 on v0

v1 whole, which is shorter than its diff:
```python
import functools
import math

import jax
import jax.numpy as jnp
from jax import lax
from jax.experimental import pallas as pl
from jax.experimental.pallas import tpu as pltpu
from jax.sharding import PartitionSpec as P

eps = 1e-06
both = ("sph", "grp")
f32 = jnp.float32
bf16 = jnp.bfloat16
masked = -8192.0
log2e = 1.4426950408889634
heads = 8
head = 64
width = 512
listed = 16
tile = 256
in_vmem = pl.BlockSpec(memory_space=pltpu.VMEM)
in_smem = pl.BlockSpec(memory_space=pltpu.SMEM)
anywhere = pl.BlockSpec(memory_space=pl.ANY)


def iota(shape, dim):
    return lax.broadcasted_iota(jnp.int32, shape, dim)


def dot(left, right):
    return jnp.dot(left, right, preferred_element_type=f32)


def dot_t(left, right):
    return lax.dot_general(left, right, (((1,), (1,)), ((), ())), preferred_element_type=f32)


def head_mean_matrix():
    same = (iota((256, 256), 0) // head) == (iota((256, 256), 1) // head)
    return jnp.where(same, 1.0 / head, 0.0).astype(bf16)


def head_mean(values, averaging):
    squares = (values * values).astype(bf16)
    return jnp.concatenate(
        [dot(squares[:, :256], averaging), dot(squares[:, 256:], averaging)], axis=1
    )


def queries(state, gain, probe, averaging):
    mean_square = jnp.mean(state * state, axis=-1, keepdims=True)
    raw = dot((state * gain).astype(bf16), probe)
    return (raw * lax.rsqrt(head_mean(raw, averaging) + eps * (mean_square + eps))).astype(bf16)


def normalize(values, gain):
    return values * lax.rsqrt(jnp.mean(values * values, axis=-1, keepdims=True) + eps) * gain


def score_scale(scales, tier):
    lane_head = iota((1, width), 1) // head
    row = jnp.zeros((1, width), f32)
    for h in range(heads):
        row = jnp.where(lane_head == h, scales[tier, h], row)
    return row * (log2e / math.sqrt(head))


def keys_values(latents, tier, expand, shrink, address, content, gains, scales, averaging):
    base = latents.astype(f32)
    hidden = dot(normalize(base, gains[tier, 1:2, :]).astype(bf16), expand)
    hidden = (hidden * (0.5 + 0.5 * jnp.tanh(0.5 * hidden))).astype(bf16)
    renewed = (base + dot(hidden, shrink)).astype(bf16).astype(f32)
    kv_in = normalize(renewed, gains[tier, 2:3, :]).astype(bf16)
    key_part = dot(kv_in, address)
    key_part = key_part * lax.rsqrt(head_mean(key_part, averaging) + eps)
    key_part = (key_part * score_scale(scales, tier)).astype(bf16)
    return key_part, dot(kv_in, content).astype(bf16)


def log_counts(places, rows):
    blocks = places.shape[0]
    doubled = jnp.concatenate([places, places], axis=0).astype(f32).astype(bf16)
    eye = (iota((listed, listed), 0) == iota((listed, listed), 1)).astype(f32).astype(bf16)
    turned = dot_t(eye, doubled)
    latent = iota((rows, 2 * blocks), 0).astype(f32)
    count = jnp.zeros((rows, 2 * blocks), f32)
    for j in range(listed):
        count = count + jnp.where(turned[j : j + 1, :] == latent, 1.0, 0.0)
    logs = jnp.where(count > 0.5, jnp.log(jnp.maximum(count, 1.0)) * log2e, masked)
    high = logs.astype(bf16).astype(f32)
    lane = iota((rows, 2 * blocks), 1)
    return jnp.where(lane < blocks, high, logs - high).astype(bf16)


def block_onehot(first_row, rows, blocks, per_block):
    block = (iota((rows, 2 * blocks), 0) + first_row) // per_block
    return (block == iota((rows, 2 * blocks), 1) % blocks).astype(f32).astype(bf16)


def first_queries_kernel(x_hbm, probe_hbm, gains, q_ref, x_buf, probe_buf, sems):
    rows = x_buf.shape[0]
    steps = rows // tile
    copies = [pltpu.make_async_copy(probe_hbm.at[0], probe_buf, sems.at[steps])]
    for t in range(steps):
        part = pl.ds(t * tile, tile)
        copies.append(pltpu.make_async_copy(x_hbm.at[part], x_buf.at[part], sems.at[t]))
    for copy in copies:
        copy.start()
    averaging = head_mean_matrix()
    copies[0].wait()
    for t in range(steps):
        copies[t + 1].wait()
        part = pl.ds(t * tile, tile)
        q_ref[part, :] = queries(
            x_buf[part, :].astype(f32), gains[0, 0:1, :], probe_buf[...], averaging
        )


def first_queries(x, probe, gains):
    rows = x.shape[0]
    return pl.pallas_call(
        first_queries_kernel,
        name="first_queries",
        out_shape=jax.ShapeDtypeStruct((rows, width), bf16),
        in_specs=[anywhere, anywhere, in_vmem],
        out_specs=in_vmem,
        scratch_shapes=[
            pltpu.VMEM((rows, width), bf16),
            pltpu.VMEM((width, width), bf16),
            pltpu.SemaphoreType.DMA((rows // tile + 1,)),
        ],
        cost_estimate=pl.CostEstimate(
            flops=2 * rows * width * width * 2, bytes_accessed=4 << 20, transcendentals=rows * width
        ),
    )(x, probe, gains)


def first_table_kernel(
    low, own, high, expand, shrink, address, content, gains, scales, k_ref, v_ref, e, s, a, c, sems
):
    copies = [
        pltpu.make_async_copy(source.at[0], target, sems.at[i])
        for i, (source, target) in enumerate(
            ((expand, e), (shrink, s), (address, a), (content, c))
        )
    ]
    for copy in copies:
        copy.start()
    averaging = head_mean_matrix()
    latents = jnp.concatenate([low[...], own[...], high[...]], axis=0)
    for copy in copies:
        copy.wait()
    k_ref[...], v_ref[...] = keys_values(
        latents, 0, e[...], s[...], a[...], c[...], gains, scales, averaging
    )


def first_table(low, own, high, expand, shrink, address, content, gains, scales):
    rows = 3 * own.shape[0]
    hidden = expand.shape[2]
    return pl.pallas_call(
        first_table_kernel,
        name="first_table",
        out_shape=[jax.ShapeDtypeStruct((rows, width), bf16)] * 2,
        in_specs=[in_vmem] * 3 + [anywhere] * 4 + [in_vmem, in_smem],
        out_specs=[in_vmem] * 2,
        scratch_shapes=[
            pltpu.VMEM((width, hidden), bf16),
            pltpu.VMEM((hidden, width), bf16),
            pltpu.VMEM((width, width), bf16),
            pltpu.VMEM((width, width), bf16),
            pltpu.SemaphoreType.DMA((4,)),
        ],
        cost_estimate=pl.CostEstimate(
            flops=16 * rows * width * hidden, bytes_accessed=8 << 20, transcendentals=rows * hidden
        ),
    )(low, own, high, expand, shrink, address, content, gains, scales)


def first_mix_kernel(
    first_row, x_hbm, q_ref, k_ref, v_ref, picks, merge_hbm, s_ref, x_buf, merge, kx, vx, sems
):
    rows = s_ref.shape[0]
    table = k_ref.shape[0]
    blocks = picks.shape[0]
    copies = [
        pltpu.make_async_copy(x_hbm.at[pl.ds(first_row, rows)], x_buf, sems.at[0]),
        pltpu.make_async_copy(merge_hbm.at[0], merge, sems.at[1]),
    ]
    for copy in copies:
        copy.start()
    listing = picks[...]
    local = listing - listing[:, 0:1] + iota(listing.shape, 0) + blocks
    logs = log_counts(local, table)
    lane = iota((table, 128), 1)
    zero = jnp.zeros((table, 128), bf16)
    left = jnp.where(lane < head, 1.0, 0.0).astype(bf16)
    right = jnp.where(lane >= head, 1.0, 0.0).astype(bf16)
    for p in range(heads // 2):
        lanes = slice(128 * p, 128 * p + 128)
        k, v = k_ref[:, lanes], v_ref[:, lanes]
        for i, side in enumerate((left, right)):
            part = pl.ds(i * table, table)
            kx[p, part, 0:128] = jnp.where(side > zero, k, zero)
            kx[p, part, 128:256] = logs
            vx[p, part, 0:128] = jnp.where(side > zero, v, zero)
            vx[p, part, 128:256] = side
    for copy in copies:
        copy.wait()

    def step(t, carry):
        part = pl.ds(pl.multiple_of(t * tile, tile), tile)
        onehot = block_onehot(first_row + t * tile, tile, blocks, 16)
        mixed = []
        for p in range(heads // 2):
            q = q_ref[pl.ds(pl.multiple_of(first_row + t * tile, tile), tile), 128 * p : 128 * p + 128]
            scores = dot_t(jnp.concatenate([q, onehot], axis=1), kx[p])
            sums = dot(jnp.exp2(scores).astype(bf16), vx[p])
            mixed.append((sums[:, :128] / sums[:, 128:]).astype(bf16))
        s_ref[part, :] = x_buf[part, :].astype(f32) + dot(
            jnp.concatenate(mixed, axis=1), merge[...]
        )
        return carry

    lax.fori_loop(0, rows // tile, step, 0)


def first_mix(x, q, k, v, picks, merge, first_row, rows):
    table = k.shape[0]
    return pl.pallas_call(
        functools.partial(first_mix_kernel, first_row),
        name="first_mix",
        out_shape=jax.ShapeDtypeStruct((rows, width), f32),
        in_specs=[anywhere, in_vmem, in_vmem, in_vmem, in_vmem, anywhere],
        out_specs=in_vmem,
        scratch_shapes=[
            pltpu.VMEM((rows, width), bf16),
            pltpu.VMEM((width, width), bf16),
            pltpu.VMEM((heads // 2, 2 * table, 256), bf16),
            pltpu.VMEM((heads // 2, 2 * table, 256), bf16),
            pltpu.SemaphoreType.DMA((2,)),
        ],
        cost_estimate=pl.CostEstimate(
            flops=rows * width * width * 14, bytes_accessed=4 << 20, transcendentals=rows * 1536
        ),
    )(x, q, k, v, picks, merge)


def coarse_kernel(
    state_a,
    state_b,
    tables,
    picks_two,
    picks_three,
    place,
    probe_hbm,
    address_hbm,
    content_hbm,
    merge_hbm,
    expand_hbm,
    shrink_hbm,
    gains,
    scales,
    out_ref,
    probe,
    address,
    content,
    merge,
    expand,
    shrink,
    kx,
    vm,
    sems,
):
    blocks = picks_two.shape[0]
    latents = tables.shape[1]
    half = state_a.shape[0]
    columns = heads * latents
    copies = []
    for i in range(2):
        for j, (source, target) in enumerate(
            (
                (expand_hbm, expand),
                (shrink_hbm, shrink),
                (address_hbm, address),
                (content_hbm, content),
                (merge_hbm, merge),
                (probe_hbm, probe),
            )
        ):
            copies.append(
                pltpu.make_async_copy(source.at[i + 1], target.at[i], sems.at[6 * i + j])
            )
    for copy in copies:
        copy.start()
    averaging = head_mean_matrix()
    group, core = place[0, 0], place[0, 1]
    two = (picks_two[...] & (latents - 1)) ^ (group << 2)
    raw = picks_three[...]
    source_group = ((raw >> 2) & 3) * 2 + (raw >> 4)
    three = ((source_group ^ group) << 2) | ((raw & 3) ^ (core << 1))
    own_head = iota((columns, width), 0) // latents == iota((columns, width), 1) // head
    zero = jnp.zeros((columns, width), bf16)
    for i, places in enumerate((two, three)):
        logs = log_counts(places, latents)
        for copy in copies[6 * i : 6 * i + 5]:
            copy.wait()
        k, v = keys_values(
            tables[i], i + 1, expand[i], shrink[i], address[i], content[i], gains, scales, averaging
        )
        kx[i, :, 0:width] = jnp.where(own_head, jnp.concatenate([k] * heads, axis=0), zero)
        kx[i, :, width : width + 128] = jnp.concatenate([logs] * heads, axis=0)
        vm[i] = dot(
            jnp.where(own_head, jnp.concatenate([v] * heads, axis=0), zero), merge[i]
        ).astype(bf16)
    copies[5].wait()
    copies[11].wait()
    same = iota((columns, columns), 0) // latents == iota((columns, columns), 1) // latents
    summing = jnp.where(same, 1.0, 0.0).astype(bf16)

    for n, state_ref in enumerate((state_a, state_b)):

        def step(t, carry, n=n, state_ref=state_ref):
            part = pl.ds(pl.multiple_of(t * tile, tile), tile)
            onehot = block_onehot(n * half + t * tile, tile, blocks, 16)
            state = state_ref[part, :]
            for i in range(2):
                q = queries(state, gains[i + 1, 0:1, :], probe[i], averaging)
                scores = dot_t(jnp.concatenate([q, onehot], axis=1), kx[i])
                powers = jnp.exp2(scores)
                weights = (powers / dot(powers.astype(bf16), summing)).astype(bf16)
                state = state + dot(weights, vm[i])
            out_ref[pl.ds(pl.multiple_of(n * half + t * tile, tile), tile), :] = state.astype(bf16)
            return carry

        lax.fori_loop(0, half // tile, step, 0)


def coarse(
    state_a, state_b, tables, two, three, place, probe, address, content, merge, expand, shrink, gains, scales
):
    rows = 2 * state_a.shape[0]
    hidden = expand.shape[2]
    columns = heads * tables.shape[1]
    square = pltpu.VMEM((2, width, width), bf16)
    return pl.pallas_call(
        coarse_kernel,
        name="coarse",
        out_shape=jax.ShapeDtypeStruct((rows, width), bf16),
        in_specs=[in_vmem] * 5 + [in_smem] + [anywhere] * 6 + [in_vmem, in_smem],
        out_specs=in_vmem,
        scratch_shapes=[
            square,
            square,
            square,
            square,
            pltpu.VMEM((2, width, hidden), bf16),
            pltpu.VMEM((2, hidden, width), bf16),
            pltpu.VMEM((2, columns, width + 128), bf16),
            pltpu.VMEM((2, columns, width), bf16),
            pltpu.SemaphoreType.DMA((12,)),
        ],
        cost_estimate=pl.CostEstimate(
            flops=rows * width * width * 12, bytes_accessed=12 << 20, transcendentals=rows * 2048
        ),
    )(
        state_a, state_b, tables, two, three, place, probe, address, content, merge, expand, shrink, gains, scales
    )


def turn_pairs(flip):
    pairs = []
    for y_hi in range(2):
        for x in range(4):
            for core in range(2):
                for z in range(4):
                    for y_lo in range(2):
                        target = (y_hi * 8 + x * 2 + core) * 8 + z * 2 + y_lo
                        source = (y_lo * 8 + z * 2 + (core ^ flip)) * 8 + x * 2 + y_hi
                        pairs.append((source, target))
    return pairs


def per_device(
    pixel_features,
    tier_one_codes,
    tier_two_codes,
    tier_three_codes,
    tier_one_picks,
    tier_two_picks,
    tier_three_picks,
    probe_matrix,
    address_matrix,
    content_matrix,
    merge_matrix,
    expand_matrix,
    shrink_matrix,
    rescale_factors,
    logit_scaling,
):
    devices = lax.axis_size(both)
    members = lax.axis_size("grp")
    forward = [(i, i + 1) for i in range(devices - 1)]
    backward = [(i + 1, i) for i in range(devices - 1)]
    low = lax.ppermute(tier_one_codes, both, forward)
    high = lax.ppermute(tier_one_codes, both, backward)
    near = lax.ppermute(tier_three_codes, both, turn_pairs(0))
    far = lax.ppermute(tier_three_codes, both, turn_pairs(1))
    q = first_queries(pixel_features, probe_matrix, rescale_factors)
    tables = jnp.stack([tier_two_codes, jnp.concatenate([near, far], axis=0)], axis=0)
    for k in (1, 2, 4):
        tables = jnp.concatenate(
            [tables, lax.ppermute(tables, "grp", [(i, i ^ k) for i in range(members)])], axis=1
        )
    k, v = first_table(
        low,
        tier_one_codes,
        high,
        expand_matrix,
        shrink_matrix,
        address_matrix,
        content_matrix,
        rescale_factors,
        logit_scaling,
    )
    half = pixel_features.shape[0] // 2
    state_a = first_mix(pixel_features, q, k, v, tier_one_picks, merge_matrix, 0, half)
    state_b = first_mix(pixel_features, q, k, v, tier_one_picks, merge_matrix, half, half)
    place = jnp.stack([lax.axis_index("grp"), lax.axis_index("sph") % 2]).reshape(1, 2)
    return coarse(
        state_a,
        state_b,
        tables,
        tier_two_picks,
        tier_three_picks,
        place.astype(jnp.int32),
        probe_matrix,
        address_matrix,
        content_matrix,
        merge_matrix,
        expand_matrix,
        shrink_matrix,
        rescale_factors,
        logit_scaling,
    )


def solution(mesh):
    placed = (
        P(both, None),
        P(both, None),
        P(both, None),
        P("sph", None),
        P(both, None),
        P(both, None),
        P(both, None),
        P(),
        P(),
        P(),
        P(),
        P(),
        P(),
        P(),
        P(),
    )
    return jax.shard_map(
        per_device, mesh=mesh, in_specs=placed, out_specs=P(both, None), check_vma=False
    )
```

time: 175 us -> 71.1 us (0.41)
  local copies, waits for them, and re-layouts: 62.3 us -> 3.34 us
  blocking collectives: 56.7 us -> 0 us
  matrix products: 37.9 us -> 0 us
  Pallas kernels: 0 us -> 35 us
  starting transfers between devices: 4.89 us -> 27.6 us
  other arithmetic: 11 us -> 3.4 us
    all_gather x2 -> x0, blocking collectives: 56.7 us -> none  [the longest x1 31.6 us: per_device(): lax.all_gather(project(renewed_two, 1, address_matrix, content_matrix, re...]
    gather x6 -> x0, local copies, waits for them, and re-layouts: 45.6 us -> none  [the longest x3 22.8 us: mix_across_tiers(): key_picked = jnp.take(key_heads, tier_positions, axis=1)]
    pallas_call x0 -> x5, Pallas kernels: none -> 35 us  [the longest x1 14.7 us: coarse(): pl.pallas_call(coarse_kernel, name='coarse', out_shape=jax.ShapeDtypeStru...]
    dot_general x18 -> x0, matrix products: 31.8 us -> none  [the longest x3 9.67 us: mix_across_tiers(): jnp.einsum('hbid,hbjd->hbij', queries, key_picked, preferred_element_type...]
    ppermute x2 -> x7, starting transfers between devices: 4.89 us -> 27.6 us  [the longest x3 23 us: per_device(): lax.ppermute(tables, 'grp', [(i, i ^ k) for i in range(members)])]
    unnamed x3 -> x0, matrix products: 6.07 us -> none
    convert_element_type x9 -> x0, local copies, waits for them, and re-layouts: 5.58 us -> none  [the longest x3 3.97 us: mix_across_tiers(): queries.astype(jnp.bfloat16)]
    slice x7 -> x0, local copies, waits for them, and re-layouts: 4.52 us -> none  [the longest x1 2.66 us: mix_across_tiers(): merge_matrix[tier_ordinal].reshape(channel_groups, group_dimension, feature)]
  transfers between devices with their start and end apart: 2 -> 7, of which waited for: 0 -> 1; matrix products, arithmetic and copies ran while one was open for 31% -> 7% of each run, Pallas kernels for 0% -> 7%
where the time goes in v1:
time: 71.1 us; the launch traced here: 70.6 us
  Pallas kernels  35 us (49%)
  starting transfers between devices  27.6 us (39%)
  other arithmetic  3.4 us (5%)
  local copies, waits for them, and re-layouts  3.34 us (5%)
  waiting for transfers between devices  1.13 us (2%)
    ppermute x3, starting transfers between devices, per_device(): lax.ppermute(tables, 'grp', [(i, i ^ k) for i in range(members)])  23 us
    pallas_call x1, Pallas kernels, coarse(): pl.pallas_call(coarse_kernel, name='coarse', out_shape=jax.ShapeDtypeStru...  14.7 us
    pallas_call x2, Pallas kernels, first_mix(): pl.pallas_call(functools.partial(first_mix_kernel, first_row), name='firs...  10.9 us
    pallas_call x1, Pallas kernels, first_queries(): pl.pallas_call(first_queries_kernel, name='first_queries', out_shape=jax....  4.73 us
    pallas_call x1, Pallas kernels, first_table(): pl.pallas_call(first_table_kernel, name='first_table', out_shape=[jax.Sha...  4.71 us
    unnamed x15, local copies, waits for them, and re-layouts  3.34 us
    concatenate x3, other arithmetic, per_device(): jnp.concatenate([tables, lax.ppermute(tables, 'grp', [(i, i ^ k) for i in...  2.04 us
    ppermute x1, starting transfers between devices, per_device(): low = lax.ppermute(tier_one_codes, both, forward)  1.92 us
  transfers between devices with their start and end apart: 7, of which 1 were waited for; matrix products, arithmetic and copies ran while one was open for 7% of the time, Pallas kernels for 7%

profile of v1, /device:TPU:0, one launch (start us, length us, event | category | flops | bytes accessed | tf_op | source)
XLA Modules:
  0.0 70.6 jit_solution(14081743154244559982)
XLA Ops:
  0.0 0.0 collective-permute-start.3
  0.0 1.3 %collective-permute-start.2 = (bf16[2,512]{1,0:T(2,128)(2,1)}, bf16[2,512]{1,0:T(2,128)(2,1)S(1)}, u32[]{:S(2)}, u32[]{:S(2)}) collective-permute-start(bf16[2,512]{1,0:T(2,128)(2,1)} %param.18), channel_id=1, source_target_pairs={{0,0},{64,1},{16,2},{80,3},{32,4},{96,5},{48,6},{112,7},{8,8},{72,... | collective-permute-start | bytes 6152 | tf_op jit(solution)/shard_map/ppermute | solution.py:408
  1.3 0.0 collective-permute-done.3
  1.4 0.0 collective-permute-done.2
  1.4 0.7 pad_maximum_fusion.3
  2.1 7.1 %collective-permute-start.4 = (bf16[2,4,512]{2,1,0:T(4,128)(2,1)S(1)}, bf16[2,4,512]{2,1,0:T(4,128)(2,1)S(1)}, u32[]{:S(2)}, u32[]{:S(2)}) collective-permute-start(bf16[2,4,512]{2,1,0:T(4,128)(2,1)S(1)} %pad_maximum_fusion.3), channel_id=1, source_target_pairs={{0,1},{1,0},{2,3},{3,2},{4,5},{5,4},{6,7},{7,6},{8,9},{9,8},{10,11... | collective-permute-start | bytes 24584 | tf_op jit(solution)/shard_map/ppermute | solution.py:414
  9.2 1.9 %collective-permute-start = (bf16[64,512]{1,0:T(8,128)(2,1)}, bf16[64,512]{1,0:T(8,128)(2,1)S(1)}, u32[]{:S(2)}, u32[]{:S(2)}) collective-permute-start(bf16[64,512]{1,0:T(8,128)(2,1)} %own.1), channel_id=1, source_target_pairs={{0,1},{1,2},{2,3},{3,4},{4,5},{5,6},{6,7},{7,8},{8,9},{9,10},{10,1... | collective-permute-start | bytes 196616 | tf_op jit(solution)/shard_map/ppermute | solution.py:406
  11.1 1.3 %collective-permute-start.1 = (bf16[64,512]{1,0:T(8,128)(2,1)}, bf16[64,512]{1,0:T(8,128)(2,1)S(1)}, u32[]{:S(2)}, u32[]{:S(2)}) collective-permute-start(bf16[64,512]{1,0:T(8,128)(2,1)} %own.1), channel_id=1, source_target_pairs={{1,0},{2,1},{3,2},{4,3},{5,4},{6,5},{7,6},{8,7},{9,8},{10,9},{11,1... | collective-permute-start | bytes 196616 | tf_op jit(solution)/shard_map/ppermute | solution.py:407
  12.4 0.0 collective-permute-done.4
  12.4 0.7 pad_maximum_fusion.2
  13.1 7.8 %collective-permute-start.5 = (bf16[2,8,512]{2,1,0:T(8,128)(2,1)S(1)}, bf16[2,8,512]{2,1,0:T(8,128)(2,1)S(1)}, u32[]{:S(2)}, u32[]{:S(2)}) collective-permute-start(bf16[2,8,512]{2,1,0:T(8,128)(2,1)S(1)} %pad_maximum_fusion.2), channel_id=1, source_target_pairs={{0,2},{1,3},{2,0},{3,1},{4,6},{5,7},{6,4},{7,5},{8,10},{9,11},{10,... | collective-permute-start | bytes 49160 | tf_op jit(solution)/shard_map/ppermute | solution.py:414
  20.9 0.6 add_bitcast_fusion.place
  21.6 1.1 %collective-permute-done.5 = bf16[2,8,512]{2,1,0:T(8,128)(2,1)S(1)} collective-permute-done((bf16[2,8,512]{2,1,0:T(8,128)(2,1)S(1)}, bf16[2,8,512]{2,1,0:T(8,128)(2,1)S(1)}, u32[]{:S(2)}, u32[]{:S(2)}) %collective-permute-start.5) | collective-permute-done | bytes 16416 | tf_op jit(solution)/shard_map/ppermute | solution.py:414
  22.6 0.7 pad_maximum_fusion.1
  23.3 0.0 copy-start.3
  23.4 0.0 copy-start.4
  23.4 0.0 copy-start.5
  23.4 0.0 copy-start.2
  23.4 8.1 %collective-permute-start.6 = (bf16[2,16,512]{2,1,0:T(8,128)(2,1)S(1)}, bf16[2,16,512]{2,1,0:T(8,128)(2,1)S(1)}, u32[]{:S(2)}, u32[]{:S(2)}) collective-permute-start(bf16[2,16,512]{2,1,0:T(8,128)(2,1)S(1)} %pad_maximum_fusion.1), channel_id=1, source_target_pairs={{0,4},{1,5},{2,6},{3,7},{4,0},{5,1},{6,2},{7,3},{8,12},{9,13},{10,... | collective-permute-start | bytes 98312 | tf_op jit(solution)/shard_map/ppermute | solution.py:414
  31.5 4.7 %first_queries.1.q_ref = bf16[1024,512]{1,0:T(8,128)(2,1)} custom-call(bf16[1024,512]{1,0:T(8,128)(2,1)} %x_hbm.5, bf16[3,512,512]{2,1,0:T(8,128)(2,1)} %probe_hbm.3, f32[3,3,512]{2,1,0:T(4,128)} %gains.5), custom_call_target="tpu_custom_call" | custom-call | flops 1073741824 | bytes 4194304 | tf_op jit(solution)/shard_map/first_queries/pallas_call | solution.py:122
  36.3 0.0 copy-done.3
  36.3 0.7 copy.16.picks
  37.0 0.0 copy-done.4
  37.0 0.7 copy.18.picks_two
  37.7 0.0 copy-done.5
  37.7 0.7 copy.19.picks_three
  38.4 0.0 collective-permute-done.6
  38.4 0.0 copy-done.2
  38.4 0.6 pad_maximum_fusion.tables
  39.0 0.0 collective-permute-done.low
  39.0 0.0 copy-start
  39.0 0.0 collective-permute-done.1.high
  39.0 0.6 copy-done
  39.6 0.0 copy-start.1
  39.6 0.6 copy-done.1
  40.3 4.7 %first_table.1 = (bf16[192,512]{1,0:T(8,128)(2,1)}, bf16[192,512]{1,0:T(8,128)(2,1)}) custom-call(bf16[64,512]{1,0:T(8,128)(2,1)} %copy-done, bf16[64,512]{1,0:T(8,128)(2,1)} %own.1, bf16[64,512]{1,0:T(8,128)(2,1)} %copy-done.1, bf16[3,512,1024]{2,1,0:T(8,128)(2,1)} %expand_hbm.1, bf16[3,1024,512]{2,1,0:T(8,128)(2,1)} %shrink_hbm.1, ...), custom_call_target="tpu_custom_call" | custom-call | flops 1610612736 | bytes 8388608 | tf_op jit(solution)/shard_map/first_table/pallas_call | solution.py:162
  45.0 5.4 %first_mix.2.state_a = f32[512,512]{1,0:T(8,128)} custom-call(bf16[1024,512]{1,0:T(8,128)(2,1)} %x_hbm.5, bf16[1024,512]{1,0:T(8,128)(2,1)} %first_queries.1.q_ref, bf16[192,512]{1,0:T(8,128)(2,1)} %get-tuple-element.7.k_ref, bf16[192,512]{1,0:T(8,128)(2,1)} %get-tuple-element.8.v_ref, s32[64,16]{1,0:T(8,128)} %copy.16.picks, bf16[3,512,512]{2,1,0:T(8,128)(2,1)} %merge_hbm.5), custom_call_target="tpu_custom_call" | custom-call | flops 1879048192 | bytes 4194304 | tf_op jit(solution)/shard_map/first_mix/pallas_call | solution.py:231
  50.4 5.5 %first_mix.3.state_b = f32[512,512]{1,0:T(8,128)} custom-call(bf16[1024,512]{1,0:T(8,128)(2,1)} %x_hbm.5, bf16[1024,512]{1,0:T(8,128)(2,1)} %first_queries.1.q_ref, bf16[192,512]{1,0:T(8,128)(2,1)} %get-tuple-element.7.k_ref, bf16[192,512]{1,0:T(8,128)(2,1)} %get-tuple-element.8.v_ref, s32[64,16]{1,0:T(8,128)} %copy.16.picks, bf16[3,512,512]{2,1,0:T(8,128)(2,1)} %merge_hbm.5), custom_call_target="tpu_custom_call" | custom-call | flops 1879048192 | bytes 4194304 | tf_op jit(solution)/shard_map/first_mix/pallas_call | solution.py:231
  55.9 14.7 %coarse.1 = bf16[1024,512]{1,0:T(8,128)(2,1)} custom-call(f32[512,512]{1,0:T(8,128)} %first_mix.2.state_a, f32[512,512]{1,0:T(8,128)} %first_mix.3.state_b, bf16[2,32,512]{2,1,0:T(8,128)(2,1)} %pad_maximum_fusion.tables, s32[64,16]{1,0:T(8,128)} %copy.18.picks_two, s32[64,16]{1,0:T(8,128)} %copy.19.picks_three, s32[1,2]{1,0:T(1,128)} %add_bitcast_fusion.place, ...), custom_call_target="tpu_custom_call" | custom-call | flops 3221225472 | bytes 12582912 | tf_op jit(solution)/shard_map/coarse/pallas_call | solution.py:347
  (1 shorter events, 0.0 us)
Async XLA Ops:
  0.0 1.4 %collective-permute-start.3 = (bf16[2,512]{1,0:T(2,128)(2,1)}, bf16[2,512]{1,0:T(2,128)(2,1)S(1)}, u32[]{:S(2)}, u32[]{:S(2)}) collective-permute-start(bf16[2,512]{1,0:T(2,128)(2,1)} %param.18), channel_id=1, source_target_pairs={{8,0},{72,1},{24,2},{88,3},{40,4},{104,5},{56,6},{120,7},{0,8},{64... | collective-permute-start | bytes 6152 | tf_op jit(solution)/shard_map/ppermute | solution.py:409
  0.0 1.4 %collective-permute-start.2 = (bf16[2,512]{1,0:T(2,128)(2,1)}, bf16[2,512]{1,0:T(2,128)(2,1)S(1)}, u32[]{:S(2)}, u32[]{:S(2)}) collective-permute-start(bf16[2,512]{1,0:T(2,128)(2,1)} %param.18), channel_id=1, source_target_pairs={{0,0},{64,1},{16,2},{80,3},{32,4},{96,5},{48,6},{112,7},{8,8},{72,... | collective-permute-start | bytes 6152 | tf_op jit(solution)/shard_map/ppermute | solution.py:408
  2.1 10.3 %collective-permute-start.4 = (bf16[2,4,512]{2,1,0:T(4,128)(2,1)S(1)}, bf16[2,4,512]{2,1,0:T(4,128)(2,1)S(1)}, u32[]{:S(2)}, u32[]{:S(2)}) collective-permute-start(bf16[2,4,512]{2,1,0:T(4,128)(2,1)S(1)} %pad_maximum_fusion.3), channel_id=1, source_target_pairs={{0,1},{1,0},{2,3},{3,2},{4,5},{5,4},{6,7},{7,6},{8,9},{9,8},{10,11... | collective-permute-start | bytes 24584 | tf_op jit(solution)/shard_map/ppermute | solution.py:414
  9.2 29.8 %collective-permute-start = (bf16[64,512]{1,0:T(8,128)(2,1)}, bf16[64,512]{1,0:T(8,128)(2,1)S(1)}, u32[]{:S(2)}, u32[]{:S(2)}) collective-permute-start(bf16[64,512]{1,0:T(8,128)(2,1)} %own.1), channel_id=1, source_target_pairs={{0,1},{1,2},{2,3},{3,4},{4,5},{5,6},{6,7},{7,8},{8,9},{9,10},{10,1... | collective-permute-start | bytes 196616 | tf_op jit(solution)/shard_map/ppermute | solution.py:406
  11.1 27.9 %collective-permute-start.1 = (bf16[64,512]{1,0:T(8,128)(2,1)}, bf16[64,512]{1,0:T(8,128)(2,1)S(1)}, u32[]{:S(2)}, u32[]{:S(2)}) collective-permute-start(bf16[64,512]{1,0:T(8,128)(2,1)} %own.1), channel_id=1, source_target_pairs={{1,0},{2,1},{3,2},{4,3},{5,4},{6,5},{7,6},{8,7},{9,8},{10,9},{11,1... | collective-permute-start | bytes 196616 | tf_op jit(solution)/shard_map/ppermute | solution.py:407
  13.1 9.5 %collective-permute-start.5 = (bf16[2,8,512]{2,1,0:T(8,128)(2,1)S(1)}, bf16[2,8,512]{2,1,0:T(8,128)(2,1)S(1)}, u32[]{:S(2)}, u32[]{:S(2)}) collective-permute-start(bf16[2,8,512]{2,1,0:T(8,128)(2,1)S(1)} %pad_maximum_fusion.2), channel_id=1, source_target_pairs={{0,2},{1,3},{2,0},{3,1},{4,6},{5,7},{6,4},{7,5},{8,10},{9,11},{10,... | collective-permute-start | bytes 49160 | tf_op jit(solution)/shard_map/ppermute | solution.py:414
  23.3 12.9 %copy-start.3 = (s32[64,16]{0,1:T(8,128)S(1)}, s32[64,16]{0,1:T(8,128)}, u32[]{:S(2)}) copy-start(s32[64,16]{0,1:T(8,128)} %param.19) | copy-start | bytes 12292
  23.4 13.6 %copy-start.4 = (s32[64,16]{0,1:T(8,128)S(1)}, s32[64,16]{0,1:T(8,128)}, u32[]{:S(2)}) copy-start(s32[64,16]{0,1:T(8,128)} %param.20) | copy-start | bytes 12292
  23.4 14.3 %copy-start.5 = (s32[64,16]{0,1:T(8,128)S(1)}, s32[64,16]{0,1:T(8,128)}, u32[]{:S(2)}) copy-start(s32[64,16]{0,1:T(8,128)} %param.21) | copy-start | bytes 12292
  23.4 15.0 %copy-start.2 = (bf16[4,512]{1,0:T(4,128)(2,1)S(1)}, bf16[4,512]{1,0:T(4,128)(2,1)}, u32[]{:S(2)}) copy-start(bf16[4,512]{1,0:T(4,128)(2,1)} %param.17) | copy-start | bytes 12292
  23.4 15.0 %collective-permute-start.6 = (bf16[2,16,512]{2,1,0:T(8,128)(2,1)S(1)}, bf16[2,16,512]{2,1,0:T(8,128)(2,1)S(1)}, u32[]{:S(2)}, u32[]{:S(2)}) collective-permute-start(bf16[2,16,512]{2,1,0:T(8,128)(2,1)S(1)} %pad_maximum_fusion.1), channel_id=1, source_target_pairs={{0,4},{1,5},{2,6},{3,7},{4,0},{5,1},{6,2},{7,3},{8,12},{9,13},{10,... | collective-permute-start | bytes 98312 | tf_op jit(solution)/shard_map/ppermute | solution.py:414
  39.0 0.6 copy-start
  39.6 0.6 copy-start.1
